TPU v7x, 32 devices: a whole 2x2x4 slice. The times are simulated.
32 devices in a mesh: wide: 16 (over z, x, core), narrow: 2 (over y).
Axes of the slice: x: 2, y: 2, z: 4, core: 2. Of those that a mesh axis runs over, the one named last changes fastest.
Arguments:
- activations: float32 [1024, 17408], P('wide', 'narrow'), may hold values from -6 to 6
- act_basis: float32 [17408, 17408], P('narrow', 'wide'), may hold values from -0.046875 to 0.046875
- grads: float32 [1024, 5120], P(None, 'wide'), may hold values from -0.3 to 0.3
- grad_basis: float32 [5120, 5120], P('wide', 'narrow'), may hold values from -0.078125 to 0.078125
- seq_ids: int32 [1024], replicated, may hold values from 0 to 3, never falling along the last dimension, each value on 1 to 512 neighbouring positions
Outputs:
- eigenvalues: float32 [17408, 5120], P('wide', 'narrow')
Inputs may be any that keep to these rules, and one draw needn't show every extreme that they name: `seq_ids`: never falling along the rows; every sequence has at least one row and at most 512 rows, and one sequence has exactly 512.
All inputs are finite; a program needn't handle non-finite values.
Results may differ from a plain program's by a relative error of at most 0.0003.
Values sent between devices are 32-bit elements; how exact they have to be, the bound alone decides.
A program may use at most 192 MiB of HBM per device.

v0:
```python
import jax
import jax.numpy as jnp
from jax import lax
from jax.sharding import PartitionSpec as P

SEQS = 4
SEQ_MOST = 512


def seq_window(rotated_acts, rotated_grads, seq_ids, seq_label):
    token_rows = rotated_grads.shape[0]
    first_row = jnp.sum((seq_ids < seq_label).astype(jnp.int32))
    window_start = jnp.minimum(first_row, token_rows - SEQ_MOST)
    acts_window = lax.dynamic_slice_in_dim(rotated_acts, window_start, SEQ_MOST, 0)
    grads_window = lax.dynamic_slice_in_dim(rotated_grads, window_start, SEQ_MOST, 0)
    ids_window = lax.dynamic_slice_in_dim(seq_ids, window_start, SEQ_MOST, 0)
    seq_mask = (ids_window == seq_label).astype(jnp.float32)[:, None]
    return (acts_window, grads_window * seq_mask)


def per_device(activations, act_basis, grads, grad_basis, seq_ids):
    highest = lax.Precision.HIGHEST
    partial_acts = jnp.dot(
        lax.all_gather(activations, "wide", axis=0, tiled=True),
        act_basis,
        precision=highest,
        preferred_element_type=jnp.float32,
    )
    rotated_acts = lax.psum(partial_acts, "narrow")
    partial_grads = jnp.dot(
        grads, grad_basis, precision=highest, preferred_element_type=jnp.float32
    )
    rotated_grads = lax.psum(partial_grads, "wide")
    out_cols = rotated_grads.shape[1]
    running = jnp.zeros((rotated_acts.shape[1], out_cols), jnp.float32)
    for seq_label in range(SEQS):
        acts_window, grads_window = seq_window(rotated_acts, rotated_grads, seq_ids, seq_label)
        moment = jnp.dot(
            acts_window.T, grads_window, precision=highest, preferred_element_type=jnp.float32
        )
        running = running + moment * moment
    return running / jnp.float32(SEQS)


def solution(mesh):
    in_specs = (P("wide", "narrow"), P("narrow", "wide"), P(None, "wide"), P("wide", "narrow"), P())
    out_specs = P("wide", "narrow")
    return jax.shard_map(
        per_device, mesh=mesh, in_specs=in_specs, out_specs=out_specs, check_vma=False
    )
```

profile of v0, /device:TPU:0, one launch (start us, length us, event | category | flops | bytes accessed | tf_op | source)
XLA Modules:
  0.0 607.1 jit_solution(9304746979321440647)
XLA Ops:
  6.5 0.0 copy-start
  6.5 0.0 all-gather.2.cloned.1.call-start
  6.5 0.7 all-gather.2.cloned.1.call-update
  7.3 0.0 all-reduce.5.cloned.1.call-start
  7.3 1.2 copy-done
  8.5 20.3 %fusion.29 = f32[1024,2560]{1,0:T(8,128)} fusion(f32[1024,320]{0,1:T(8,128)} %param.7, f32[320,2560]{1,0:T(8,128)S(1)} %copy-done), kind=kOutput, calls=%fused_computation.41 | convolution fusion | flops 10066329600 | bytes 15073280 | tf_op jit(solution)/shard_map/dot_general | solution.py:30
  28.8 0.0 all-reduce.5.cloned.1.call-update
  28.8 0.0 copy-start.3
  28.8 0.6 all-reduce.3.cloned.1.call-start
  29.4 160.2 %all-gather.2.cloned.1.call-done = f32[1024,8704]{1,0:T(8,128)} async-done(((f32[64,8704]{1,0:T(8,128)}), f32[1024,8704]{1,0:T(8,128)}) %all-gather.2.cloned.1.call-update) | async-done | bytes 35651600 | tf_op jit(solution)/shard_map/all_gather | solution.py:24
  189.6 127.6 %fusion.28 = f32[1024,1088]{0,1:T(8,128)} fusion(f32[1024,8704]{1,0:T(8,128)} %all-gather.2.cloned.1.call-done, f32[8704,1088]{0,1:T(8,128)} %param.6), kind=kOutput, calls=%fused_computation.40 | convolution fusion | flops 116366770176 | bytes 77987840 | tf_op jit(solution)/shard_map/dot_general | solution.py:23
  317.2 0.0 all-reduce.3.cloned.1.call-update
  317.3 0.0 copy-done.3
  317.3 0.7 convert_reduce_fusion
  320.5 0.1 fusion.27
  320.6 73.7 %all-reduce.5.cloned.1.call-done = f32[1024,2560]{1,0:T(8,128)} async-done(((f32[1024,2560]{1,0:T(8,128)}), f32[1024,2560]{1,0:T(8,128)}) %all-reduce.5.cloned.1.call-update) | async-done | bytes 10485776 | tf_op jit(solution)/shard_map/psum | solution.py:33
  394.3 116.0 %all-reduce.3.cloned.1.call-done = f32[1024,1088]{0,1:T(8,128)} async-done(((f32[1024,1088]{0,1:T(8,128)}), f32[1024,1088]{0,1:T(8,128)}) %all-reduce.3.cloned.1.call-update) | async-done | bytes 4456464 | tf_op jit(solution)/shard_map/psum | solution.py:29
  510.4 0.0 copy-start.2
  510.4 22.4 %convolution_multiply_fusion.2 = f32[1088,2560]{1,0:T(8,128)S(1)} fusion(f32[1024,2560]{1,0:T(8,128)} %all-reduce.5.cloned.1.call-done, s32[]{:T(128)S(6)} %select_n.9, f32[512]{0:T(512)S(1)} %get-tuple-element.12, f32[1024,1088]{0,1:T(8,128)} %all-reduce.3.cloned.1.call-done), kind=kOutput, calls=%fused_computation.2 | convolution fusion | flops 17116856320 | bytes 18615296 | tf_op jit(solution)/shard_map/dot_general | solution.py:38
  532.7 0.0 copy-done.2
  532.7 21.9 %fusion = f32[1088,2560]{1,0:T(8,128)S(1)} fusion(f32[1088,2560]{1,0:T(8,128)S(1)} %convolution_multiply_fusion.2, f32[1024,2560]{1,0:T(8,128)} %all-reduce.5.cloned.1.call-done, s32[]{:T(128)S(6)} %select_n.8, f32[512]{0:T(512)S(1)} %get-tuple-element.11, f32[1024,1088]{0,1:T(8,128)S(1)} %copy-done.2), kind=kOutput, calls=%fused_computation.4 | convolution fusion | flops 17119641600 | bytes 29756416 | tf_op jit(solution)/shard_map/dot_general | solution.py:38
  554.7 21.9 %fusion.1 = f32[1088,2560]{1,0:T(8,128)S(1)} fusion(f32[1088,2560]{1,0:T(8,128)S(1)} %fusion, f32[1024,2560]{1,0:T(8,128)} %all-reduce.5.cloned.1.call-done, s32[]{:T(128)S(6)} %select_n.10, f32[512]{0:T(512)S(1)} %get-tuple-element.10, f32[1024,1088]{0,1:T(8,128)S(1)} %copy-done.2), kind=kOutput, calls=%fused_computation.5 | convolution fusion | flops 17119641600 | bytes 29756416 | tf_op jit(solution)/shard_map/dot_general | solution.py:38
  576.6 0.0 copy-start.1
  576.6 23.4 %fusion.3 = f32[1088,2560]{1,0:T(8,128)} fusion(f32[1088,2560]{1,0:T(8,128)S(1)} %fusion.1, f32[1024,2560]{1,0:T(8,128)} %all-reduce.5.cloned.1.call-done, s32[]{:T(128)S(6)} %select_n.11, f32[512]{0:T(512)S(1)} %get-tuple-element.9, f32[1024,1088]{0,1:T(8,128)S(1)} %copy-done.2), kind=kOutput, calls=%fused_computation.7 | convolution fusion | flops 17122426880 | bytes 29756416 | tf_op jit(solution)/shard_map/dot_general | solution.py:38
  600.0 0.0 copy-done.1
Async XLA Ops:
  6.5 1.9 copy-start
  6.5 183.1 %all-gather.2.cloned.1.call-start = ((), (), s32[]{:S(2)}) async-start(), calls=%async_computation | async-start | bytes 37879808 | tf_op jit(solution)/shard_map/all_gather | solution.py:24
  7.3 387.1 %all-reduce.5.cloned.1.call-start = ((), (), s32[]{:S(2)}) async-start(), calls=%async_computation.2 | async-start | bytes 20971520 | tf_op jit(solution)/shard_map/psum | solution.py:33
  28.8 288.4 %copy-start.3 = (s32[1024]{0:T(1024)S(1)}, s32[1024]{0:T(1024)}, u32[]{:S(2)}) copy-start(s32[1024]{0:T(1024)} %param.9) | copy-start | bytes 12292
  28.8 481.5 %all-reduce.3.cloned.1.call-start = ((), (), s32[]{:S(2)}) async-start(), calls=%async_computation.1 | async-start | bytes 8912896 | tf_op jit(solution)/shard_map/psum | solution.py:29
  510.4 22.4 %copy-start.2 = (f32[1024,1088]{0,1:T(8,128)S(1)}, f32[1024,1088]{0,1:T(8,128)}, u32[]{:S(2)}) copy-start(f32[1024,1088]{0,1:T(8,128)} %all-reduce.3.cloned.1.call-done) | copy-start | bytes 13369348
  576.6 23.4 %copy-start.1 = (f32[320,2560]{1,0:T(8,128)S(1)}, f32[320,2560]{1,0:T(8,128)}, u32[]{:S(2)}) copy-start(f32[320,2560]{1,0:T(8,128)} %param.8) | copy-start | bytes 9830404
Sparse Core Ops, SparseCore 0:
  8.9 180.6 all-gather.1
  193.4 200.9 all-reduce.4
  396.8 113.5 all-reduce.2
where the time goes:
time: 614 us; the launch traced here: 607 us
  waiting for transfers between devices  351 us (57%)
  matrix products  238 us (39%)
  between operations  16.2 us (3%)
    all_gather x1, waiting for transfers between devices, per_device(): lax.all_gather(activations, 'wide', axis=0, tiled=True)  160 us
    dot_general x1, matrix products, per_device(): jnp.dot(lax.all_gather(activations, 'wide', axis=0, tiled=True), act_basi...  128 us
    psum x1, waiting for transfers between devices, per_device(): rotated_acts = lax.psum(partial_acts, 'narrow')  116 us
    dot_general x4, matrix products, per_device(): jnp.dot(acts_window.T, grads_window, precision=highest, preferred_element...  89.6 us
    psum x1, waiting for transfers between devices, per_device(): rotated_grads = lax.psum(partial_grads, 'wide')  73.7 us
    dot_general x1, matrix products, per_device(): jnp.dot(grads, grad_basis, precision=highest, preferred_element_type=jnp....  20.3 us
  transfers between devices with their start and end apart: 3, of which 3 were waited for; matrix products, arithmetic and copies ran while one was open for 25% of the time, Pallas kernels for 0%

commit v1 on v0

--- a/solution.py
+++ b/solution.py
@@ -30,7 +30,11 @@
     partial_grads = jnp.dot(
         grads, grad_basis, precision=highest, preferred_element_type=jnp.float32
     )
-    rotated_grads = lax.psum(partial_grads, "wide")
+    rotated_grads = partial_grads
+    for hop in (1, 2, 4, 8):
+        rotated_grads = rotated_grads + lax.ppermute(
+            rotated_grads, "wide", [(dev, dev ^ hop) for dev in range(16)]
+        )
     out_cols = rotated_grads.shape[1]
     running = jnp.zeros((rotated_acts.shape[1], out_cols), jnp.float32)
     for seq_label in range(SEQS):

time: 614 us -> 1240 us (2.02)
  waiting for transfers between devices: 351 us -> 913 us
  other arithmetic: 0.8 us -> 54.8 us
    ppermute x0 -> x4, waiting for transfers between devices: none -> 912 us  [per_device(): lax.ppermute(rotated_grads, 'wide', [(dev, dev ^ hop) for dev in range(16)])]
    all_gather x1, waiting for transfers between devices: 160 us -> 0.01 us  [per_device(): lax.all_gather(activations, 'wide', axis=0, tiled=True)]
    psum x1, waiting for transfers between devices: 116 us -> 0.01 us  [per_device(): rotated_acts = lax.psum(partial_acts, 'narrow')]
    psum x1 -> x0, waiting for transfers between devices: 73.7 us -> none  [per_device(): rotated_grads = lax.psum(partial_grads, 'wide')]
    add x0 -> x4, other arithmetic: none -> 53.9 us  [per_device(): rotated_grads + lax.ppermute(rotated_grads, 'wide', [(dev, dev ^ hop) for...]
  transfers between devices with their start and end apart: 3 -> 6, of which waited for: 3 -> 4; matrix products, arithmetic and copies ran while one was open for 25% -> 16% of each run, Pallas kernels for 0% -> 0%
where the time goes in v1:
time: 1240 us; the launch traced here: 1230 us
  waiting for transfers between devices  913 us (74%)
  matrix products  241 us (19%)
  other arithmetic  54.8 us (4%)
  between operations  16.5 us (1%)
    ppermute x4, waiting for transfers between devices, per_device(): lax.ppermute(rotated_grads, 'wide', [(dev, dev ^ hop) for dev in range(16)])  912 us
    dot_general x1, matrix products, per_device(): jnp.dot(lax.all_gather(activations, 'wide', axis=0, tiled=True), act_basi...  128 us
    dot_general x4, matrix products, per_device(): jnp.dot(acts_window.T, grads_window, precision=highest, preferred_element...  95.1 us
    add x4, other arithmetic, per_device(): rotated_grads + lax.ppermute(rotated_grads, 'wide', [(dev, dev ^ hop) for...  53.9 us
  transfers between devices with their start and end apart: 6, of which 4 were waited for; matrix products, arithmetic and copies ran while one was open for 16% of the time, Pallas kernels for 0%

profile of v1, /device:TPU:0, one launch (start us, length us, event | category | flops | bytes accessed | tf_op | source)
XLA Modules:
  0.0 1235.0 jit_solution(5611039043959261798)
XLA Ops:
  6.5 0.0 copy-start
  6.5 0.0 all-gather.2.cloned.1.call-start
  6.5 0.7 all-gather.2.cloned.1.call-update
  7.3 0.0 all-reduce.2.cloned.1.call-start
  7.3 1.2 copy-done
  8.5 18.1 %fusion.29 = f32[1024,2560]{1,0:T(8,128)S(1)} fusion(f32[1024,320]{0,1:T(8,128)} %param.7, f32[320,2560]{1,0:T(8,128)S(1)} %copy-done), kind=kOutput, calls=%fused_computation.41 | convolution fusion | flops 10066329600 | bytes 15073280 | tf_op jit(solution)/shard_map/dot_general | solution.py:30
  26.6 0.0 copy-start.2
  26.6 4.1 copy-done.2
  30.7 0.5 collective-permute-start
  31.2 18.3 %collective-permute-done = f32[1024,2560]{1,0:T(8,128)} collective-permute-done((f32[1024,2560]{1,0:T(8,128)S(1)}, f32[1024,2560]{1,0:T(8,128)}, u32[]{:S(2)}, u32[]{:S(2)}) %collective-permute-start) | collective-permute-done | bytes 10485792 | tf_op jit(solution)/shard_map/ppermute | solution.py:35
  49.5 13.7 %add.44 = f32[1024,2560]{1,0:T(8,128)} add(f32[1024,2560]{1,0:T(8,128)} %copy-done.2, f32[1024,2560]{1,0:T(8,128)} %collective-permute-done) | non-fusion elementwise | flops 2621440 | bytes 31457280 | tf_op jit(solution)/shard_map/add | solution.py:35
  63.2 2.2 collective-permute-start.1
  65.3 346.8 %collective-permute-done.1 = f32[1024,2560]{1,0:T(8,128)} collective-permute-done((f32[1024,2560]{1,0:T(8,128)}, f32[1024,2560]{1,0:T(8,128)}, u32[]{:S(2)}, u32[]{:S(2)}) %collective-permute-start.1) | collective-permute-done | bytes 10485792 | tf_op jit(solution)/shard_map/ppermute | solution.py:35
  412.1 13.3 %add.45 = f32[1024,2560]{1,0:T(8,128)} add(f32[1024,2560]{1,0:T(8,128)} %add.44, f32[1024,2560]{1,0:T(8,128)} %collective-permute-done.1) | non-fusion elementwise | flops 2621440 | bytes 31457280 | tf_op jit(solution)/shard_map/add | solution.py:35
  425.5 0.0 collective-permute-start.2
  425.5 227.7 %collective-permute-done.2 = f32[1024,2560]{1,0:T(8,128)} collective-permute-done((f32[1024,2560]{1,0:T(8,128)}, f32[1024,2560]{1,0:T(8,128)}, u32[]{:S(2)}, u32[]{:S(2)}) %collective-permute-start.2) | collective-permute-done | bytes 10485792 | tf_op jit(solution)/shard_map/ppermute | solution.py:35
  653.1 13.7 %add.46 = f32[1024,2560]{1,0:T(8,128)} add(f32[1024,2560]{1,0:T(8,128)} %add.45, f32[1024,2560]{1,0:T(8,128)} %collective-permute-done.2) | non-fusion elementwise | flops 2621440 | bytes 31457280 | tf_op jit(solution)/shard_map/add | solution.py:35
  666.9 2.0 collective-permute-start.3
  668.9 127.7 %fusion.28 = f32[1024,1088]{0,1:T(8,128)} fusion(f32[1024,8704]{1,0:T(8,128)} %all-gather.2.cloned.1.call-done, f32[8704,1088]{0,1:T(8,128)} %param.6), kind=kOutput, calls=%fused_computation.40 | convolution fusion | flops 116366770176 | bytes 77987840 | tf_op jit(solution)/shard_map/dot_general | solution.py:23
  796.5 0.0 all-reduce.2.cloned.1.call-update
  796.6 0.0 copy-done.3
  796.6 0.7 convert_reduce_fusion.3
  799.8 0.1 fusion.24
  799.9 319.4 %collective-permute-done.3 = f32[1024,2560]{1,0:T(8,128)} collective-permute-done((f32[1024,2560]{1,0:T(8,128)}, f32[1024,2560]{1,0:T(8,128)}, u32[]{:S(2)}, u32[]{:S(2)}) %collective-permute-start.3) | collective-permute-done | bytes 10485792 | tf_op jit(solution)/shard_map/ppermute | solution.py:35
  1119.3 13.2 %add.47 = f32[1024,2560]{1,0:T(8,128)} add(f32[1024,2560]{1,0:T(8,128)} %add.46, f32[1024,2560]{1,0:T(8,128)} %collective-permute-done.3) | non-fusion elementwise | flops 2621440 | bytes 31457280 | tf_op jit(solution)/shard_map/add | solution.py:35
  1132.5 0.0 slice-start.2
  1132.5 0.0 slice-start.4
  1132.5 24.0 %convolution_multiply_fusion = f32[1088,2560]{1,0:T(8,128)} fusion(f32[1024,2560]{1,0:T(8,128)} %add.47, s32[]{:T(128)S(6)} %select_n.11, f32[512]{0:T(512)S(1)} %get-tuple-element.11, f32[1024,1088]{0,1:T(8,128)} %all-reduce.2.cloned.1.call-done), kind=kOutput, calls=%fused_computation | convolution fusion | flops 17116856320 | bytes 18615296 | tf_op jit(solution)/shard_map/dot_general | solution.py:42
  1156.5 21.6 %convolution_multiply_fusion.1 = f32[1088,2560]{1,0:T(8,128)} fusion(f32[1024,2560]{1,0:T(8,128)S(1)} %bitcast.5, s32[]{:T(128)S(6)} %select_n.10, f32[512]{0:T(512)S(1)} %get-tuple-element.10, f32[1024,1088]{0,1:T(8,128)S(1)} %bitcast.7), kind=kOutput, calls=%fused_computation.1 | convolution fusion | flops 17116856320 | bytes 18615296 | tf_op jit(solution)/shard_map/dot_general | solution.py:42
  1178.2 21.5 %convolution_multiply_fusion.2 = f32[1088,2560]{1,0:T(8,128)} fusion(f32[1024,2560]{1,0:T(8,128)S(1)} %bitcast.5, s32[]{:T(128)S(6)} %select_n.9, f32[512]{0:T(512)S(1)} %get-tuple-element.12, f32[1024,1088]{0,1:T(8,128)S(1)} %bitcast.7), kind=kOutput, calls=%fused_computation.2 | convolution fusion | flops 17116856320 | bytes 18615296 | tf_op jit(solution)/shard_map/dot_general | solution.py:42
  1199.6 28.0 %fusion.3 = f32[1088,2560]{1,0:T(8,128)} fusion(f32[1088,2560]{1,0:T(8,128)} %convolution_multiply_fusion, f32[1088,2560]{1,0:T(8,128)} %convolution_multiply_fusion.1, f32[1088,2560]{1,0:T(8,128)} %convolution_multiply_fusion.2, f32[1024,2560]{1,0:T(8,128)} %add.47, s32[]{:T(128)S(6)} %select_n.8, f32[512]{0:T(512)S(1)} %get-tuple-element.9, ...), kind=kOutput, calls=%fused_computation.7 | convolution fusion | flops 17127997440 | bytes 52038656 | tf_op jit(solution)/shard_map/dot_general | solution.py:42
  1227.6 0.0 copy-done.1
  (14 shorter events, 0.0 us)
Async XLA Ops:
  6.5 1.9 copy-start
  6.5 662.3 %all-gather.2.cloned.1.call-start = ((), (), s32[]{:S(2)}) async-start(), calls=%async_computation | async-start | bytes 37879808 | tf_op jit(solution)/shard_map/all_gather | solution.py:24
  7.3 1125.2 %all-reduce.2.cloned.1.call-start = ((), (), s32[]{:S(2)}) async-start(), calls=%async_computation.1 | async-start | bytes 8912896 | tf_op jit(solution)/shard_map/psum | solution.py:29
  26.6 4.1 copy-start.2
  30.7 18.8 %collective-permute-start = (f32[1024,2560]{1,0:T(8,128)S(1)}, f32[1024,2560]{1,0:T(8,128)}, u32[]{:S(2)}, u32[]{:S(2)}) collective-permute-start(f32[1024,2560]{1,0:T(8,128)S(1)} %fusion.29), channel_id=1, source_target_pairs={{0,2},{2,0},{4,6},{6,4},{8,10},{10,8},{12,14},{14,12},{16,18},{18,... | collective-permute-start | bytes 31457288 | tf_op jit(solution)/shard_map/ppermute | solution.py:35
  63.2 349.0 %collective-permute-start.1 = (f32[1024,2560]{1,0:T(8,128)}, f32[1024,2560]{1,0:T(8,128)}, u32[]{:S(2)}, u32[]{:S(2)}) collective-permute-start(f32[1024,2560]{1,0:T(8,128)} %add.44), channel_id=1, source_target_pairs={{0,4},{2,6},{4,0},{6,2},{8,12},{10,14},{12,8},{14,10},{16,20},{18,... | collective-permute-start | bytes 31457288 | tf_op jit(solution)/shard_map/ppermute | solution.py:35
  425.5 227.7 %collective-permute-start.2 = (f32[1024,2560]{1,0:T(8,128)}, f32[1024,2560]{1,0:T(8,128)}, u32[]{:S(2)}, u32[]{:S(2)}) collective-permute-start(f32[1024,2560]{1,0:T(8,128)} %add.45), channel_id=1, source_target_pairs={{0,8},{2,10},{4,12},{6,14},{8,0},{10,2},{12,4},{14,6},{16,24},{18,... | collective-permute-start | bytes 31457288 | tf_op jit(solution)/shard_map/ppermute | solution.py:35
  666.9 129.7 %copy-start.3 = (s32[1024]{0:T(1024)S(1)}, s32[1024]{0:T(1024)}, u32[]{:S(2)}) copy-start(s32[1024]{0:T(1024)} %param.9) | copy-start | bytes 12292
  666.9 452.4 %collective-permute-start.3 = (f32[1024,2560]{1,0:T(8,128)}, f32[1024,2560]{1,0:T(8,128)}, u32[]{:S(2)}, u32[]{:S(2)}) collective-permute-start(f32[1024,2560]{1,0:T(8,128)} %add.46), channel_id=1, source_target_pairs={{0,16},{2,18},{4,20},{6,22},{8,24},{10,26},{12,28},{14,30},{16,0},... | collective-permute-start | bytes 31457288 | tf_op jit(solution)/shard_map/ppermute | solution.py:35
  1132.4 24.0 %slice-start = ((s8[10485760]{0:T(1024)(128)(4,1)}), s8[4194304]{0:T(1024)(128)(4,1)S(1)}, s32[]{:S(2)}) async-start(s8[10485760]{0:T(1024)(128)(4,1)} %bitcast.4), calls=%async_computation.2 | async-start | bytes 8388608
  1132.5 24.0 %slice-start.3 = ((s8[4456448]{0:T(1024)(128)(4,1)}), s8[4194304]{0:T(1024)(128)(4,1)S(1)}, s32[]{:S(2)}) async-start(s8[4456448]{0:T(1024)(128)(4,1)} %bitcast.6), calls=%async_computation.5 | async-start | bytes 8388608
  1132.5 24.0 %slice-start.1 = ((s8[10485760]{0:T(1024)(128)(4,1)}), s8[4194304]{0:T(1024)(128)(4,1)S(1)}, s32[]{:S(2)}) async-start(s8[10485760]{0:T(1024)(128)(4,1)} %bitcast.4), calls=%async_computation.3 | async-start | bytes 8388608
  1132.5 24.0 %slice-start.2 = ((s8[10485760]{0:T(1024)(128)(4,1)}), s8[2097152]{0:T(1024)(128)(4,1)S(1)}, s32[]{:S(2)}) async-start(s8[10485760]{0:T(1024)(128)(4,1)} %bitcast.4), calls=%async_computation.4 | async-start | bytes 4194304
  1132.5 24.0 %slice-start.4 = ((s8[4456448]{0:T(1024)(128)(4,1)}), s8[262144]{0:T(1024)(128)(4,1)S(1)}, s32[]{:S(2)}) async-start(s8[4456448]{0:T(1024)(128)(4,1)} %bitcast.6), calls=%async_computation.6 | async-start | bytes 524288
  1199.6 28.0 %copy-start.1 = (f32[320,2560]{1,0:T(8,128)S(1)}, f32[320,2560]{1,0:T(8,128)}, u32[]{:S(2)}) copy-start(f32[320,2560]{1,0:T(8,128)} %param.8) | copy-start | bytes 9830404
Sparse Core Ops, SparseCore 0:
  8.9 300.9 all-gather.1
  796.7 111.9 all-reduce.1
